TPU v7x, 32 devices: a whole 2x2x4 slice. The times are simulated.
32 devices in a mesh: cp: 4 (over y, x), fsdp: 2 (over core), rep: 4 (over z).
Axes of the slice: x: 2, y: 2, z: 4, core: 2. Of those that a mesh axis runs over, the one named last changes fastest.
Arguments:
- tokens: bfloat16 [16, 2048, 768], P(('fsdp', 'rep'), 'cp'), may hold values from -6 to 6
- segments: int32 [16, 2048], P(('fsdp', 'rep')), may hold values from 0 to 3, never falling along the last dimension, each value on 1 to 1024 neighbouring positions
- g_one: bfloat16 [768], P('fsdp'), may hold values from 0.099609375 to 1.8984375
- b_one: bfloat16 [768], P('fsdp'), may hold values from -3 to 3
- w_qkv: bfloat16 [768, 2304], P('fsdp'), may hold values from -0.21875 to 0.21875
- b_query: bfloat16 [768], P('fsdp'), may hold values from -3 to 3
- b_value: bfloat16 [768], P('fsdp'), may hold values from -3 to 3
- w_out: bfloat16 [768, 768], P('fsdp'), may hold values from -1.75 to 1.75
- b_out: bfloat16 [768], P('fsdp'), may hold values from -3 to 3
- g_two: bfloat16 [768], P('fsdp'), may hold values from 0.099609375 to 1.8984375
- b_two: bfloat16 [768], P('fsdp'), may hold values from -3 to 3
- w_fc: bfloat16 [768, 3072], P('fsdp'), may hold values from -0.21875 to 0.21875
- b_fc: bfloat16 [3072], P('fsdp'), may hold values from -3 to 3
- w_proj: bfloat16 [3072, 768], P('fsdp'), may hold values from -0.109375 to 0.109375
- b_proj: bfloat16 [768], P('fsdp'), may hold values from -3 to 3
- cotangent: bfloat16 [16, 2048, 768], P(('fsdp', 'rep'), 'cp'), may hold values from -6 to 6
Outputs:
- layer_out: bfloat16 [16, 2048, 768], P(('fsdp', 'rep'), 'cp')
- tokens_grad: bfloat16 [16, 2048, 768], P(('fsdp', 'rep'), 'cp')
- dg_one: float32 [768], P('fsdp')
- db_one: float32 [768], P('fsdp')
- dw_qkv: float32 [768, 2304], P('fsdp')
- db_query: float32 [768], P('fsdp')
- db_value: float32 [768], P('fsdp')
- dw_out: float32 [768, 768], P('fsdp')
- db_out: float32 [768], P('fsdp')
- dg_two: float32 [768], P('fsdp')
- db_two: float32 [768], P('fsdp')
- dw_fc: float32 [768, 3072], P('fsdp')
- db_fc: float32 [3072], P('fsdp')
- dw_proj: float32 [3072, 768], P('fsdp')
- db_proj: float32 [768], P('fsdp')
Inputs may be any that keep to these rules, and one draw needn't show every extreme that they name: `segments`: in each sequence the ids never fall, and each document holds 1 to 1024 positions, one document exactly that many.
All inputs are finite; a program needn't handle non-finite values.
Results may differ from a plain program's by a relative error of at most 0.012.
The roundings to bfloat16 on the way count: a program that leaves them out, or rounds other values in their place, can miss the bound.
Values may be sent and summed in bfloat16 or wider, within the bound.
A program may use at most 384 MiB of HBM per device.

v0:
```python
import jax
import jax.numpy as jnp
from jax import lax
from jax.sharding import PartitionSpec as P

HEADS = 12


def layer_norm(value, gain, shift):
    center = value - jnp.mean(value, axis=-1, keepdims=True)
    spread = jnp.mean(center * center, axis=-1, keepdims=True)
    return center * lax.rsqrt(spread + 1e-05) * gain + shift


def gelu_tanh(value):
    return (
        0.5
        * value
        * (1.0 + jnp.tanh(0.7978845608028654 * (value + 0.044715 * value * value * value)))
    )


def inner_rows(left, right):
    return lax.dot_general(
        left, right, (((0,), (0,)), ((), ())), preferred_element_type=jnp.float32
    )


def times_trans(left, right):
    return lax.dot_general(
        left, right, (((1,), (1,)), ((), ())), preferred_element_type=jnp.float32
    )


def body(
    tokens,
    segments,
    g_one,
    b_one,
    w_qkv,
    b_query,
    b_value,
    w_out,
    b_out,
    g_two,
    b_two,
    w_fc,
    b_fc,
    w_proj,
    b_proj,
    cotangent,
):
    seqs, span, width = tokens.shape
    seq_len = segments.shape[1]
    rows = seqs * span
    size = width // HEADS
    scale = size ** (-0.5)
    first_pos = lax.axis_index("cp") * span
    full = (
        lax.all_gather(g_one, "fsdp", axis=0, tiled=True),
        lax.all_gather(b_one, "fsdp", axis=0, tiled=True),
        lax.all_gather(w_qkv, "fsdp", axis=0, tiled=True),
        lax.all_gather(b_query, "fsdp", axis=0, tiled=True),
        lax.all_gather(b_value, "fsdp", axis=0, tiled=True),
        lax.all_gather(w_out, "fsdp", axis=0, tiled=True),
        lax.all_gather(b_out, "fsdp", axis=0, tiled=True),
        lax.all_gather(g_two, "fsdp", axis=0, tiled=True),
        lax.all_gather(b_two, "fsdp", axis=0, tiled=True),
        lax.all_gather(w_fc, "fsdp", axis=0, tiled=True),
        lax.all_gather(b_fc, "fsdp", axis=0, tiled=True),
        lax.all_gather(w_proj, "fsdp", axis=0, tiled=True),
        lax.all_gather(b_proj, "fsdp", axis=0, tiled=True),
    )
    gain_one = full[0].astype(jnp.float32)
    shift_one = full[1].astype(jnp.float32)
    gain_two = full[7].astype(jnp.float32)
    shift_two = full[8].astype(jnp.float32)
    tok_rows = tokens.reshape(rows, width).astype(jnp.float32)
    normed = layer_norm(tok_rows, gain_one, shift_one).astype(jnp.bfloat16)
    qkv_bias = jnp.concatenate([full[3], jnp.zeros_like(full[3]), full[4]]).astype(jnp.float32)
    merged = (jnp.dot(normed, full[2], preferred_element_type=jnp.float32) + qkv_bias).astype(
        jnp.bfloat16
    )
    merged = merged.reshape(seqs, span, 3 * width)
    query = merged[:, :, :width]
    key_loc = merged[:, :, width : 2 * width]
    value_loc = merged[:, :, 2 * width :]
    keys_all, values_all = (
        lax.all_gather(key_loc, "cp", axis=1, tiled=True),
        lax.all_gather(value_loc, "cp", axis=1, tiled=True),
    )
    key_pos = jnp.arange(seq_len)

    def masked_scores(q_rows, k_rows, seq_ids, near_ids):
        length = k_rows.shape[0]
        q_three = q_rows.reshape(span, HEADS, size)
        k_three = k_rows.reshape(length, HEADS, size)
        scores = (
            jnp.einsum("qhd,khd->hqk", q_three, k_three, preferred_element_type=jnp.float32) * scale
        )
        query_ids = lax.dynamic_slice_in_dim(seq_ids, first_pos, span)
        query_pos = first_pos + jnp.arange(span)
        allowed = (query_ids[:, None] == near_ids[None, :]) & (
            key_pos[None, :] <= query_pos[:, None]
        )
        return jnp.where(allowed[None], scores, -1e30)

    def attend(item):
        q_rows, k_rows, v_rows, seq_ids, near_ids = item
        length = k_rows.shape[0]
        scores = masked_scores(q_rows, k_rows, seq_ids, near_ids)
        top = jnp.max(scores, axis=-1, keepdims=True)
        expo = jnp.exp(scores - top)
        total = jnp.sum(expo, axis=-1, keepdims=True)
        probs = (expo / total).astype(jnp.bfloat16)
        mixed = jnp.einsum(
            "hqk,khd->qhd",
            probs,
            v_rows.reshape(length, HEADS, size),
            preferred_element_type=jnp.float32,
        )
        return (
            mixed.reshape(span, width).astype(jnp.bfloat16),
            top[..., 0] + jnp.log(total[..., 0]),
        )

    mixed, log_total = lax.map(attend, (query, keys_all, values_all, segments, segments))
    mixed_rows = mixed.reshape(rows, width)
    branch = jnp.dot(mixed_rows, full[5], preferred_element_type=jnp.float32) + full[6].astype(
        jnp.float32
    )
    resid = tok_rows + branch
    normed_two = layer_norm(resid, gain_two, shift_two).astype(jnp.bfloat16)
    hidden = jnp.dot(normed_two, full[9], preferred_element_type=jnp.float32) + full[10].astype(
        jnp.float32
    )
    active = gelu_tanh(hidden).astype(jnp.bfloat16)
    output = jnp.dot(active, full[11], preferred_element_type=jnp.float32) + full[12].astype(
        jnp.float32
    )
    layer_out = (resid + output).astype(jnp.bfloat16).reshape(seqs, span, width)
    back = (
        lax.all_gather(g_one, "fsdp", axis=0, tiled=True),
        lax.all_gather(b_one, "fsdp", axis=0, tiled=True),
        lax.all_gather(w_qkv, "fsdp", axis=0, tiled=True),
        lax.all_gather(b_query, "fsdp", axis=0, tiled=True),
        lax.all_gather(b_value, "fsdp", axis=0, tiled=True),
        lax.all_gather(w_out, "fsdp", axis=0, tiled=True),
        lax.all_gather(b_out, "fsdp", axis=0, tiled=True),
        lax.all_gather(g_two, "fsdp", axis=0, tiled=True),
        lax.all_gather(b_two, "fsdp", axis=0, tiled=True),
        lax.all_gather(w_fc, "fsdp", axis=0, tiled=True),
        lax.all_gather(b_fc, "fsdp", axis=0, tiled=True),
        lax.all_gather(w_proj, "fsdp", axis=0, tiled=True),
        lax.all_gather(b_proj, "fsdp", axis=0, tiled=True),
    )
    keys_b, values_b = (
        lax.all_gather(key_loc, "cp", axis=1, tiled=True),
        lax.all_gather(value_loc, "cp", axis=1, tiled=True),
    )
    out_grad = cotangent.reshape(rows, width).astype(jnp.float32)
    d_output = out_grad.astype(jnp.bfloat16)
    dw_proj = inner_rows(active, d_output)
    db_proj = jnp.sum(d_output.astype(jnp.float32), axis=0)
    d_active = times_trans(d_output, back[11])
    _, gelu_pull = jax.vjp(gelu_tanh, hidden)
    d_hidden = gelu_pull(d_active)[0].astype(jnp.bfloat16)
    dw_fc = inner_rows(normed_two, d_hidden)
    db_fc = jnp.sum(d_hidden.astype(jnp.float32), axis=0)
    d_normed_two = times_trans(d_hidden, back[9])
    _, norm_pull_two = jax.vjp(
        layer_norm, resid, back[7].astype(jnp.float32), back[8].astype(jnp.float32)
    )
    d_resid_part, dg_two, db_two = norm_pull_two(d_normed_two)
    d_resid = out_grad + d_resid_part
    d_branch = d_resid.astype(jnp.bfloat16)
    dw_out = inner_rows(mixed_rows, d_branch)
    db_out = jnp.sum(d_branch.astype(jnp.float32), axis=0)
    d_mixed = times_trans(d_branch, back[5]).astype(jnp.bfloat16).reshape(seqs, span, width)

    def attend_back(item):
        q_rows, k_rows, v_rows, seq_ids, near_ids, d_rows, lse_rows = item
        length = k_rows.shape[0]
        scores = masked_scores(q_rows, k_rows, seq_ids, near_ids)
        probs = jnp.exp(scores - lse_rows[..., None])
        d_three = d_rows.reshape(span, HEADS, size)
        v_three = v_rows.reshape(length, HEADS, size)
        d_probs = jnp.einsum("qhd,khd->hqk", d_three, v_three, preferred_element_type=jnp.float32)
        delta = jnp.sum(probs * d_probs, axis=-1, keepdims=True)
        d_scores = (probs * (d_probs - delta)).astype(jnp.bfloat16)
        d_query = (
            jnp.einsum(
                "hqk,khd->qhd",
                d_scores,
                k_rows.reshape(length, HEADS, size),
                preferred_element_type=jnp.float32,
            )
            * scale
        )
        d_key = (
            jnp.einsum(
                "hqk,qhd->khd",
                d_scores,
                q_rows.reshape(span, HEADS, size),
                preferred_element_type=jnp.float32,
            )
            * scale
        )
        d_value = jnp.einsum(
            "hqk,qhd->khd", probs.astype(jnp.bfloat16), d_three, preferred_element_type=jnp.float32
        )
        return (
            d_query.reshape(span, width),
            d_key.reshape(length, width),
            d_value.reshape(length, width),
        )

    d_query, d_key_all, d_value_all = lax.map(
        attend_back, (query, keys_b, values_b, segments, segments, d_mixed, log_total)
    )
    d_key, d_value = (
        lax.psum_scatter(d_key_all, "cp", scatter_dimension=1, tiled=True),
        lax.psum_scatter(d_value_all, "cp", scatter_dimension=1, tiled=True),
    )
    d_merged = (
        jnp.concatenate([d_query, d_key, d_value], axis=-1)
        .astype(jnp.bfloat16)
        .reshape(rows, 3 * width)
    )
    d_merged_f = d_merged.astype(jnp.float32)
    db_query = jnp.sum(d_merged_f[:, :width], axis=0)
    db_value = jnp.sum(d_merged_f[:, 2 * width :], axis=0)
    dw_qkv = inner_rows(normed, d_merged)
    d_normed = times_trans(d_merged, back[2])
    _, norm_pull_one = jax.vjp(
        layer_norm, tok_rows, back[0].astype(jnp.float32), back[1].astype(jnp.float32)
    )
    d_tok_part, dg_one, db_one = norm_pull_one(d_normed)
    tokens_grad = (d_resid + d_tok_part).astype(jnp.bfloat16).reshape(seqs, span, width)
    shards = (
        lax.psum_scatter(dg_one, "fsdp", scatter_dimension=0, tiled=True),
        lax.psum_scatter(db_one, "fsdp", scatter_dimension=0, tiled=True),
        lax.psum_scatter(dw_qkv, "fsdp", scatter_dimension=0, tiled=True),
        lax.psum_scatter(db_query, "fsdp", scatter_dimension=0, tiled=True),
        lax.psum_scatter(db_value, "fsdp", scatter_dimension=0, tiled=True),
        lax.psum_scatter(dw_out, "fsdp", scatter_dimension=0, tiled=True),
        lax.psum_scatter(db_out, "fsdp", scatter_dimension=0, tiled=True),
        lax.psum_scatter(dg_two, "fsdp", scatter_dimension=0, tiled=True),
        lax.psum_scatter(db_two, "fsdp", scatter_dimension=0, tiled=True),
        lax.psum_scatter(dw_fc, "fsdp", scatter_dimension=0, tiled=True),
        lax.psum_scatter(db_fc, "fsdp", scatter_dimension=0, tiled=True),
        lax.psum_scatter(dw_proj, "fsdp", scatter_dimension=0, tiled=True),
        lax.psum_scatter(db_proj, "fsdp", scatter_dimension=0, tiled=True),
    )
    totals = lax.psum(
        (
            shards[0],
            shards[1],
            shards[2],
            shards[3],
            shards[4],
            shards[5],
            shards[6],
            shards[7],
            shards[8],
            shards[9],
            shards[10],
            shards[11],
            shards[12],
        ),
        ("cp", "rep"),
    )
    return (
        layer_out,
        tokens_grad,
        totals[0],
        totals[1],
        totals[2],
        totals[3],
        totals[4],
        totals[5],
        totals[6],
        totals[7],
        totals[8],
        totals[9],
        totals[10],
        totals[11],
        totals[12],
    )


def solution(mesh):
    placed = (
        P(("fsdp", "rep"), "cp", None),
        P(("fsdp", "rep"), None),
        P("fsdp"),
        P("fsdp"),
        P("fsdp", None),
        P("fsdp"),
        P("fsdp"),
        P("fsdp", None),
        P("fsdp"),
        P("fsdp"),
        P("fsdp"),
        P("fsdp", None),
        P("fsdp"),
        P("fsdp", None),
        P("fsdp"),
        P(("fsdp", "rep"), "cp", None),
    )
    return jax.shard_map(
        body,
        mesh=mesh,
        in_specs=placed,
        out_specs=(
            P(("fsdp", "rep"), "cp", None),
            P(("fsdp", "rep"), "cp", None),
            P("fsdp"),
            P("fsdp"),
            P("fsdp", None),
            P("fsdp"),
            P("fsdp"),
            P("fsdp", None),
            P("fsdp"),
            P("fsdp"),
            P("fsdp"),
            P("fsdp", None),
            P("fsdp"),
            P("fsdp", None),
            P("fsdp"),
        ),
        check_vma=False,
    )
```

profile of v0, /device:TPU:0, one launch (start us, length us, event | category | flops | bytes accessed | tf_op | source)
XLA Modules:
  0.0 1499.2 jit_solution(1097224443274911993)
XLA Ops:
  25.0 6.0 add_convert_fusion
  50.4 56.1 %all-gather.20.cloned.1.call-done = bf16[2,2048,768]{1,2,0:T(8,128)(2,1)} async-done(((bf16[2,512,768]{1,2,0:T(8,128)(2,1)}), bf16[2,2048,768]{1,2,0:T(8,128)(2,1)}) %all-gather.20.cloned.1.call-update) | async-done | bytes 6291472 | tf_op jit(solution)/shard_map/all_gather | solution.py:89
  106.5 72.5 %all-gather.18.cloned.1.call-done = bf16[2,2048,768]{1,2,0:T(8,128)(2,1)} async-done(((bf16[2,512,768]{1,2,0:T(8,128)(2,1)}), bf16[2,2048,768]{1,2,0:T(8,128)(2,1)}) %all-gather.18.cloned.1.call-update) | async-done | bytes 6291472 | tf_op jit(solution)/shard_map/all_gather | solution.py:90
  178.9 155.2 %while.34 = (s32[]{:T(128)}, bf16[2,512,768]{2,1,0:T(8,128)(2,1)}, f32[2,12,512]{2,1,0:T(8,128)S(1)}, bf16[2,2048,768]{1,2,0:T(8,128)(2,1)}, s32[2,2048]{1,0:T(2...) while((s32[]{:T(128)}, bf16[2,512,768]{2,1,0:T(8,128)(2,1)}, ...), condition=%wide.region_5.6_spmd.clone, body=%wide.region_2.5_spmd.clone.sunk | while | flops 3375753728 | bytes 197388496 | solution.py:127
  183.3 5.4 constant_dynamic-slice_fusion.17
  188.6 23.9 %fusion.106 = (f32[12,512]{1,0:T(8,128)S(1)}, f32[12,512,2048]{2,1,0:T(8,128)}) fusion(pred[512,2048]{1,0:T(8,128)(4,1)} %fusion.105, bf16[512,12,64]{0,2,1:T(8,128)(2,1)} %bitcast.170, bf16[2048,12,64]{0,2,1:T(8,128)(2,1)S(1)} %bitcast.165), kind=kOutput, calls=%fused_computation.5.clone.1 | convolution fusion | flops 1648355328 | bytes 55336960 | tf_op jit(solution)/shard_map/while/body/eval_jaxpr/qhd,khd->hqk/dot_general | solution.py:99
  212.5 24.5 %fusion.107 = f32[12,512]{1,0:T(8,128)S(1)} fusion(f32[12,512,2048]{2,1,0:T(8,128)} %get-tuple-element.683, f32[12,512]{1,0:T(8,128)S(1)} %get-tuple-element.684, pred[512,2048]{1,0:T(8,128)(4,1)} %fusion.105), kind=kLoop, calls=%fused_computation.6.clone.1 | loop fusion | flops 50325504 | bytes 51429376 | tf_op jit(solution)/shard_map/while/body/eval_jaxpr/reduce_sum | solution.py:114
  237.1 20.2 %fusion.108 = bf16[12,64,512]{2,1,0:T(8,128)(2,1)S(1)} fusion(bf16[2048,12,64]{0,2,1:T(8,128)(2,1)S(1)} %bitcast.174, f32[12,512,2048]{2,1,0:T(8,128)} %get-tuple-element.683, f32[12,512]{1,0:T(8,128)S(1)} %fusion.107, f32[12,512]{1,0:T(8,128)S(1)} %get-tuple-element.684, pred[512,2048]{1,0:T(8,128)(4,1)S(1)} %copy-done), kind=kOutput, calls=%fused_computation.10.clone.1 | convolution fusion | flops 1673920512 | bytes 55361536 | tf_op jit(solution)/shard_map/while/body/eval_jaxpr/hqk,khd->qhd/dot_general | solution.py:116
  262.8 5.4 constant_dynamic-slice_fusion.17
  268.2 21.5 %fusion.106 = (f32[12,512]{1,0:T(8,128)S(1)}, f32[12,512,2048]{2,1,0:T(8,128)}) fusion(pred[512,2048]{1,0:T(8,128)(4,1)} %fusion.105, bf16[512,12,64]{0,2,1:T(8,128)(2,1)} %bitcast.170, bf16[2048,12,64]{0,2,1:T(8,128)(2,1)S(1)} %bitcast.165), kind=kOutput, calls=%fused_computation.5.clone.1 | convolution fusion | flops 1648355328 | bytes 55336960 | tf_op jit(solution)/shard_map/while/body/eval_jaxpr/qhd,khd->hqk/dot_general | solution.py:99
  289.7 22.9 %fusion.107 = f32[12,512]{1,0:T(8,128)S(1)} fusion(f32[12,512,2048]{2,1,0:T(8,128)} %get-tuple-element.683, f32[12,512]{1,0:T(8,128)S(1)} %get-tuple-element.684, pred[512,2048]{1,0:T(8,128)(4,1)} %fusion.105), kind=kLoop, calls=%fused_computation.6.clone.1 | loop fusion | flops 50325504 | bytes 51429376 | tf_op jit(solution)/shard_map/while/body/eval_jaxpr/reduce_sum | solution.py:114
  312.5 20.2 %fusion.108 = bf16[12,64,512]{2,1,0:T(8,128)(2,1)S(1)} fusion(bf16[2048,12,64]{0,2,1:T(8,128)(2,1)S(1)} %bitcast.174, f32[12,512,2048]{2,1,0:T(8,128)} %get-tuple-element.683, f32[12,512]{1,0:T(8,128)S(1)} %fusion.107, f32[12,512]{1,0:T(8,128)S(1)} %get-tuple-element.684, pred[512,2048]{1,0:T(8,128)(4,1)S(1)} %copy-done), kind=kOutput, calls=%fused_computation.10.clone.1 | convolution fusion | flops 1673920512 | bytes 55361536 | tf_op jit(solution)/shard_map/while/body/eval_jaxpr/hqk,khd->qhd/dot_general | solution.py:116
  338.5 11.0 fusion.43
  349.5 18.8 %convert_reduce_fusion = (f32[3072]{0:T(1024)}, bf16[1024,3072]{1,0:T(8,128)(2,1)S(1)}) fusion(bf16[1024,768]{1,0:T(8,128)(2,1)} %bitcast.176, bf16[3072,768]{1,0:T(8,128)(2,1)} %all-gather.26.cloned.1.call-done, f32[1024,3072]{1,0:T(8,128)} %fusion.43, f32[3072]{0:T(1024)S(1)} %bitcast.201), kind=kOutput, calls=%fused_computation.52 | convolution fusion | flops 4916769792 | bytes 25190400 | tf_op jit(solution)/shard_map/dot_general | solution.py:30
  368.4 6.1 multiply_reduce_fusion.1
  379.7 375.4 %while.35 = (s32[]{:T(128)}, bf16[2,512,768]{2,1,0:T(8,128)(2,1)}, f32[2,2048,768]{2,1,0:T(8,128)}, f32[2,2048,768]{2,1,0:T(8,128)}, bf16[2,2048,768]{1,2,0:T(8,...) while((s32[]{:T(128)}, bf16[2,512,768]{2,1,0:T(8,128)(2,1)}, ...), condition=%wide.region_12.13_spmd.clone, body=%wide.region_10.12_spmd.clone.sunk | while | flops 8247306752 | bytes 519514368 | solution.py:218
  392.5 20.5 %fusion.119 = f32[12,512,2048]{2,1,0:T(8,128)} fusion(bf16[512,12,64]{0,2,1:T(8,128)(2,1)} %bitcast.167, bf16[2048,12,64]{0,2,1:T(8,128)(2,1)S(1)} %bitcast.162), kind=kOutput, calls=%fused_computation.114.clone.1 | convolution fusion | flops 1610612736 | bytes 54263808 | tf_op jit(solution)/shard_map/while/body/eval_jaxpr/qhd,khd->hqk/dot_general | solution.py:99
  413.0 23.1 %fusion.121 = f32[12,64,2048]{2,1,0:T(8,128)} fusion(bf16[512,12,64]{0,2,1:T(8,128)(2,1)} %bitcast.172, f32[12,512,2048]{2,1,0:T(8,128)} %fusion.119, f32[12,512]{1,0:T(8,128)S(1)} %dynamic-slice_bitcast_fusion.2, pred[512,2048]{1,0:T(8,128)(4,1)} %fusion.120), kind=kOutput, calls=%fused_computation.24.clone.1 | convolution fusion | flops 1660944384 | bytes 58482688 | tf_op jit(solution)/shard_map/while/body/eval_jaxpr/hqk,qhd->khd/dot_general | solution.py:209
  436.1 6.6 copy.90
  442.7 37.6 %multiply_reduce_fusion.5 = (f32[12,512]{1,0:T(8,128)S(1)}, f32[12,512,2048]{2,1,0:T(8,128)}) fusion(f32[12,512,2048]{2,1,0:T(8,128)} %fusion.119, f32[12,512]{1,0:T(8,128)S(1)} %dynamic-slice_bitcast_fusion.2, pred[512,2048]{1,0:T(8,128)(4,1)} %fusion.120, bf16[512,12,64]{0,2,1:T(8,128)(2,1)} %bitcast.173, bf16[2048,12,64]{0,2,1:T(8,128)(2,1)} %bitcast.166), kind=kOutput, calls=%fused_computation.21.clone.1 | convolution fusion | flops 1673521152 | bytes 105693184 | tf_op jit(solution)/shard_map/while/body/eval_jaxpr/qhd,khd->hqk/dot_general | solution.py:188
  480.3 41.4 %multiply_convert_fusion.5 = bf16[12,512,2048]{2,1,0:T(8,128)(2,1)} fusion(f32[12,512,2048]{2,1,0:T(8,128)} %get-tuple-element.697, f32[12,512,2048]{2,1,0:T(8,128)} %fusion.119, f32[12,512]{1,0:T(8,128)S(1)} %get-tuple-element.698, f32[12,512]{1,0:T(8,128)S(1)} %dynamic-slice_bitcast_fusion.2, pred[512,2048]{1,0:T(8,128)(4,1)} %fusion.120), kind=kLoop, calls=%fused_computation.20.clone.1 | loop fusion | flops 75497472 | bytes 126926848 | tf_op jit(solution)/shard_map/while/body/eval_jaxpr/convert_element_type | solution.py:190
  521.7 13.4 convolution_multiply_fusion.4
  535.1 15.5 %convolution_multiply_fusion.5 = f32[12,64,2048]{2,1,0:T(8,128)} fusion(bf16[512,12,64]{0,2,1:T(8,128)(2,1)} %bitcast.168, bf16[12,512,2048]{2,1,0:T(8,128)(2,1)} %multiply_convert_fusion.5), kind=kOutput, calls=%fused_computation.28.clone.1 | convolution fusion | flops 1612185600 | bytes 32243712 | tf_op jit(solution)/shard_map/while/body/eval_jaxpr/hqk,qhd->khd/dot_general | solution.py:201
  550.6 6.6 copy.91
  558.5 10.2 constant_dynamic-update-slice_fusion.9
  578.6 20.5 %fusion.119 = f32[12,512,2048]{2,1,0:T(8,128)} fusion(bf16[512,12,64]{0,2,1:T(8,128)(2,1)} %bitcast.167, bf16[2048,12,64]{0,2,1:T(8,128)(2,1)S(1)} %bitcast.162), kind=kOutput, calls=%fused_computation.114.clone.1 | convolution fusion | flops 1610612736 | bytes 54263808 | tf_op jit(solution)/shard_map/while/body/eval_jaxpr/qhd,khd->hqk/dot_general | solution.py:99
  599.1 23.1 %fusion.121 = f32[12,64,2048]{2,1,0:T(8,128)} fusion(bf16[512,12,64]{0,2,1:T(8,128)(2,1)} %bitcast.172, f32[12,512,2048]{2,1,0:T(8,128)} %fusion.119, f32[12,512]{1,0:T(8,128)S(1)} %dynamic-slice_bitcast_fusion.2, pred[512,2048]{1,0:T(8,128)(4,1)} %fusion.120), kind=kOutput, calls=%fused_computation.24.clone.1 | convolution fusion | flops 1660944384 | bytes 58482688 | tf_op jit(solution)/shard_map/while/body/eval_jaxpr/hqk,qhd->khd/dot_general | solution.py:209
  622.2 6.6 copy.90
  628.9 37.6 %multiply_reduce_fusion.5 = (f32[12,512]{1,0:T(8,128)S(1)}, f32[12,512,2048]{2,1,0:T(8,128)}) fusion(f32[12,512,2048]{2,1,0:T(8,128)} %fusion.119, f32[12,512]{1,0:T(8,128)S(1)} %dynamic-slice_bitcast_fusion.2, pred[512,2048]{1,0:T(8,128)(4,1)} %fusion.120, bf16[512,12,64]{0,2,1:T(8,128)(2,1)} %bitcast.173, bf16[2048,12,64]{0,2,1:T(8,128)(2,1)} %bitcast.166), kind=kOutput, calls=%fused_computation.21.clone.1 | convolution fusion | flops 1673521152 | bytes 105693184 | tf_op jit(solution)/shard_map/while/body/eval_jaxpr/qhd,khd->hqk/dot_general | solution.py:188
  666.4 41.4 %multiply_convert_fusion.5 = bf16[12,512,2048]{2,1,0:T(8,128)(2,1)} fusion(f32[12,512,2048]{2,1,0:T(8,128)} %get-tuple-element.697, f32[12,512,2048]{2,1,0:T(8,128)} %fusion.119, f32[12,512]{1,0:T(8,128)S(1)} %get-tuple-element.698, f32[12,512]{1,0:T(8,128)S(1)} %dynamic-slice_bitcast_fusion.2, pred[512,2048]{1,0:T(8,128)(4,1)} %fusion.120), kind=kLoop, calls=%fused_computation.20.clone.1 | loop fusion | flops 75497472 | bytes 126926848 | tf_op jit(solution)/shard_map/while/body/eval_jaxpr/convert_element_type | solution.py:190
  707.8 13.4 convolution_multiply_fusion.4
  721.2 15.5 %convolution_multiply_fusion.5 = f32[12,64,2048]{2,1,0:T(8,128)} fusion(bf16[512,12,64]{0,2,1:T(8,128)(2,1)} %bitcast.168, bf16[12,512,2048]{2,1,0:T(8,128)(2,1)} %multiply_convert_fusion.5), kind=kOutput, calls=%fused_computation.28.clone.1 | convolution fusion | flops 1612185600 | bytes 32243712 | tf_op jit(solution)/shard_map/while/body/eval_jaxpr/hqk,qhd->khd/dot_general | solution.py:201
  736.7 6.6 copy.91
  744.6 10.1 constant_dynamic-update-slice_fusion.9
  756.0 4.9 fusion.51
  761.0 11.6 fusion.42
  774.0 13.0 fusion.44
  787.2 88.8 %reduce-scatter.9.cloned.1.call-done = f32[2,512,768]{2,1,0:T(8,128)} async-done(((f32[2,2048,768]{2,1,0:T(8,128)}), f32[2,512,768]{2,1,0:T(8,128)}) %reduce-scatter.9.cloned.1.call-update) | async-done | bytes 3145744 | tf_op jit(solution)/shard_map/reduce_scatter | solution.py:223
  878.1 121.8 %reduce-scatter.7.cloned.1.call-done = f32[2,512,768]{2,1,0:T(8,128)} async-done(((f32[2,2048,768]{2,1,0:T(8,128)}), f32[2,512,768]{2,1,0:T(8,128)}) %reduce-scatter.7.cloned.1.call-update) | async-done | bytes 3145744 | tf_op jit(solution)/shard_map/reduce_scatter | solution.py:222
  1003.2 8.3 fusion.39
  1012.7 21.2 %reduce-scatter.15.cloned.1.call-done = f32[384,3072]{1,0:T(8,128)} async-done(((f32[768,3072]{1,0:T(8,128)}), f32[384,3072]{1,0:T(8,128)}) %reduce-scatter.15.cloned.1.call-update) | async-done | bytes 4718608 | tf_op jit(solution)/shard_map/reduce_scatter | solution.py:250
  1033.9 21.5 %reduce-scatter.17.cloned.1.call-done = f32[1536,768]{1,0:T(8,128)} async-done(((f32[3072,768]{1,0:T(8,128)}), f32[1536,768]{1,0:T(8,128)}) %reduce-scatter.17.cloned.1.call-update) | async-done | bytes 4718608 | tf_op jit(solution)/shard_map/reduce_scatter | solution.py:252
  1055.4 19.1 %reduce-scatter.11.cloned.1.call-done = f32[384,2304]{1,0:T(8,128)} async-done(((f32[768,2304]{1,0:T(8,128)}), f32[384,2304]{1,0:T(8,128)}) %reduce-scatter.11.cloned.1.call-update) | async-done | bytes 3538960 | tf_op jit(solution)/shard_map/reduce_scatter | solution.py:243
  1079.2 13.6 add_convert_fusion.2
  1092.8 5.5 fusion.45
  1108.0 82.4 %all-reduce.9 = (f32[384]{0:T(512)}, f32[384]{0:T(512)}, f32[384]{0:T(512)}, f32[384]{0:T(512)}, f32[384]{0:T(512)}, /*index=5*/f32[384]{0:T(512)}, f32[384]{0:T(512)}, f32[1536]{0:T(1024)}, f32[384]{0:T(512)}) all-reduce(f32[384]{0:T(512)S(1)} %dynamic-slice.11, ...), channel_id=1, replica_groups=mesh['cp'=4,'fsdp'=2,'rep'=4] {'cp','rep'}, use_global_device_ids=true, to_apply=%region_19.20 | all-reduce | flops 4608 | bytes 36864 | tf_op jit(solution)/shard_map/psum | solution.py:255
  1190.4 4.6 add_convert_fusion.1
  1195.0 286.7 %all-reduce.14.cloned.1.call-done = (f32[384,2304]{1,0:T(8,128)}, f32[384,768]{1,0:T(8,128)}, f32[384,3072]{1,0:T(8,128)}, f32[1536,768]{1,0:T(8,128)}) async-done(((f32[384,2304]{1,0:T(8,128)}, f32[384,768]{1,0:T(8,128)}, f32[384,3072]{1,0:T(8,128)}, f32[1536,768]{1,0:T(8,128)}), (f32[384,2304]{1,0:T(8,128)}, f32[384,768]{1,0:T(8,128)}, f32[384,3072]{1,0:T(8,128)}, ...) | async-done | bytes 14155792 | tf_op jit(solution)/shard_map/psum | solution.py:255
  (295 shorter events, 112.1 us)
Async XLA Ops:
  7.2 12.8 copy-start.4
  7.2 17.8 %all-gather.16.cloned.1.call-start = ((), (), s32[]{:S(2)}) async-start(), calls=%async_computation.6 | async-start | bytes 5308416 | tf_op jit(solution)/shard_map/all_gather | solution.py:62
  7.9 98.5 %all-gather.20.cloned.1.call-start = ((), (), s32[]{:S(2)}) async-start(), calls=%async_computation.8 | async-start | bytes 7864320 | tf_op jit(solution)/shard_map/all_gather | solution.py:89
  10.6 20.4 %copy-start.30 = (f32[768]{0:T(1024)}, f32[768]{0:T(1024)S(1)}, u32[]{:S(2)}) copy-start(f32[768]{0:T(1024)S(1)} %reshape.445) | copy-start | bytes 9220
  21.9 9.2 copy-start.19
  35.1 143.8 %all-gather.18.cloned.1.call-start = ((), (), s32[]{:S(2)}) async-start(), calls=%async_computation.7 | async-start | bytes 7864320 | tf_op jit(solution)/shard_map/all_gather | solution.py:90
  36.8 6.7 copy-start.52
  36.8 9.1 copy-start.47
  36.8 297.3 %all-gather.22.cloned.1.call-start = ((), (), s32[]{:S(2)}) async-start(), calls=%async_computation.9 | async-start | bytes 1769472 | tf_op jit(solution)/shard_map/all_gather | solution.py:65
  37.4 141.6 %copy-start.23 = (s32[2,2048]{1,0:T(2,128)S(1)}, s32[2,2048]{1,0:T(2,128)}, u32[]{:S(2)}) copy-start(s32[2,2048]{1,0:T(2,128)} %param.21) | copy-start | bytes 49156
  37.4 301.1 %all-gather.24.cloned.1.call-start = ((), (), s32[]{:S(2)}) async-start(), calls=%async_computation.10 | async-start | bytes 7077888 | tf_op jit(solution)/shard_map/all_gather | solution.py:69
  38.0 311.6 %all-gather.26.cloned.1.call-start = ((), (), s32[]{:S(2)}) async-start(), calls=%async_computation.11 | async-start | bytes 7077888 | tf_op jit(solution)/shard_map/all_gather | solution.py:71
  38.5 837.5 %reduce-scatter.9.cloned.1.call-start = ((), (), s32[]{:S(2)}) async-start(), calls=%async_computation.13 | async-start | bytes 15728640 | tf_op jit(solution)/shard_map/reduce_scatter | solution.py:223
  178.9 155.2 %copy-start.46 = (f32[768]{0:T(1024)S(1)}, f32[768]{0:T(1024)}, u32[]{:S(2)}) copy-start(f32[768]{0:T(1024)} %reshape.447) | copy-start | bytes 9220
  212.5 24.5 %copy-start = (pred[512,2048]{1,0:T(8,128)(4,1)S(1)}, pred[512,2048]{1,0:T(8,128)(4,1)}, u32[]{:S(2)}) copy-start(pred[512,2048]{1,0:T(8,128)(4,1)} %fusion.105) | copy-start | bytes 3145732 | tf_op jit(solution)/shard_map/while
  212.5 24.5 %copy-start.3 = (bf16[1,2048,768]{1,2,0:T(8,128)(2,1)S(1)}, bf16[1,2048,768]{1,2,0:T(8,128)(2,1)}, u32[]{:S(2)}) copy-start(bf16[1,2048,768]{1,2,0:T(8,128)(2,1)} %get-tuple-element.681) | copy-start | bytes 9437188 | tf_op jit(solution)/shard_map/while
  289.6 22.9 %copy-start = (pred[512,2048]{1,0:T(8,128)(4,1)S(1)}, pred[512,2048]{1,0:T(8,128)(4,1)}, u32[]{:S(2)}) copy-start(pred[512,2048]{1,0:T(8,128)(4,1)} %fusion.105) | copy-start | bytes 3145732 | tf_op jit(solution)/shard_map/while
  289.6 22.9 %copy-start.3 = (bf16[1,2048,768]{1,2,0:T(8,128)(2,1)S(1)}, bf16[1,2048,768]{1,2,0:T(8,128)(2,1)}, u32[]{:S(2)}) copy-start(bf16[1,2048,768]{1,2,0:T(8,128)(2,1)} %get-tuple-element.681) | copy-start | bytes 9437188 | tf_op jit(solution)/shard_map/while
  337.9 36.6 %copy-start.6 = (f32[1024,768]{1,0:T(8,128)}, f32[1024,768]{1,0:T(8,128)S(1)}, u32[]{:S(2)}) copy-start(f32[1024,768]{1,0:T(8,128)S(1)} %get-tuple-element.552) | copy-start | bytes 9437188
  338.0 36.6 %copy-start.24 = (f32[1024]{0:T(1024)}, f32[1024]{0:T(1024)S(1)}, u32[]{:S(2)}) copy-start(f32[1024]{0:T(1024)S(1)} %broadcast_multiply_fusion) | copy-start | bytes 12292
  338.5 36.1 %copy-start.26 = (f32[1024]{0:T(1024)}, f32[1024]{0:T(1024)S(1)}, u32[]{:S(2)}) copy-start(f32[1024]{0:T(1024)S(1)} %fusion.36) | copy-start | bytes 12292
  338.5 11.1 copy-start.43
  349.5 18.8 %copy-start.54 = (bf16[768,3072]{1,0:T(8,128)(2,1)S(1)}, bf16[768,3072]{1,0:T(8,128)(2,1)}, u32[]{:S(2)}) copy-start(bf16[768,3072]{1,0:T(8,128)(2,1)} %all-gather.24.cloned.1.call-done) | copy-start | bytes 14155780
  368.4 6.1 copy-start.14
  382.6 9.6 copy-start.12
  386.1 6.2 copy-start.1
  550.6 6.6 copy-start.2
  558.5 10.2 copy-start.13
  568.7 9.6 copy-start.12
  572.2 6.2 copy-start.1
  736.7 6.6 copy-start.2
  744.6 10.1 copy-start.13
  755.1 244.8 %reduce-scatter.7.cloned.1.call-start = ((), (), s32[]{:S(2)}) async-start(), calls=%async_computation.12 | async-start | bytes 15728640 | tf_op jit(solution)/shard_map/reduce_scatter | solution.py:222
  755.9 256.8 %reduce-scatter.13.cloned.1.call-start = ((), (), s32[]{:S(2)}) async-start(), calls=%async_computation.15 | async-start | bytes 3538944 | tf_op jit(solution)/shard_map/reduce_scatter | solution.py:246
  760.9 273.0 %reduce-scatter.15.cloned.1.call-start = ((), (), s32[]{:S(2)}) async-start(), calls=%async_computation.16 | async-start | bytes 14155776 | tf_op jit(solution)/shard_map/reduce_scatter | solution.py:250
  772.6 282.7 %reduce-scatter.17.cloned.1.call-start = ((), (), s32[]{:S(2)}) async-start(), calls=%async_computation.17 | async-start | bytes 14155776 | tf_op jit(solution)/shard_map/reduce_scatter | solution.py:252
  787.0 287.5 %reduce-scatter.11.cloned.1.call-start = ((), (), s32[]{:S(2)}) async-start(), calls=%async_computation.14 | async-start | bytes 10616832 | tf_op jit(solution)/shard_map/reduce_scatter | solution.py:243
  878.1 133.4 %copy-start.15 = (bf16[2,512,768]{2,1,0:T(8,128)(2,1)}, bf16[2,512,768]{2,1,0:T(8,128)(2,1)S(1)}, u32[]{:S(2)}) copy-start(bf16[2,512,768]{2,1,0:T(8,128)(2,1)S(1)} %convert.15) | copy-start | bytes 4718596
  1011.5 470.1 %all-reduce.14.cloned.1.call-start = ((), (), s32[]{:S(2)}) async-start(), calls=%async_computation.18 | async-start | bytes 28311552 | tf_op jit(solution)/shard_map/psum | solution.py:255
  1079.2 13.6 copy-start.5
  1079.2 13.6 copy-start.16
  1079.2 13.6 copy-start.18
  1079.2 13.6 copy-start.31
  1079.2 13.6 copy-start.35
  1079.2 13.6 copy-start.55
  1092.8 5.5 copy-start.41
  1101.7 88.7 %copy-start.39 = (f32[1024]{0:T(1024)S(1)}, f32[1024]{0:T(1024)}, u32[]{:S(2)}) copy-start(f32[1024]{0:T(1024)} %copy-done.38) | copy-start | bytes 12292
  1481.7 5.2 slice-start.2
  (33 other events, 95.5 us)
Sparse Core Ops, SparseCore 0:
  9.6 15.3 all-gather.15
  35.2 71.1 all-gather.19
  108.9 70.0 all-gather.17
  180.3 9.2 all-gather.21
  191.0 15.5 all-gather.23
  208.0 15.6 all-gather.25
  755.2 120.7 reduce-scatter.8
  879.2 120.7 reduce-scatter.6
  1002.8 9.8 reduce-scatter.12
  1014.9 18.9 reduce-scatter.14
  1036.3 19.0 reduce-scatter.16
  1057.7 16.8 reduce-scatter.10
  1081.0 400.6 all-reduce.13
where the time goes:
time: 1500 us
  waiting for transfers between devices  695 us (46%)
  matrix products  410 us (27%)
  other arithmetic  160 us (11%)
  local copies, waits for them, and re-layouts  111 us (7%)
  blocking collectives  103 us (7%)
  between operations  16.3 us (1%)
    psum x1, waiting for transfers between devices, body(): lax.psum((shards[0], shards[1], shards[2], shards[3], shards[4], shards[5...  287 us
    reduce_scatter x1, waiting for transfers between devices, body(): lax.psum_scatter(d_key_all, 'cp', scatter_dimension=1, tiled=True)  122 us
    reduce_scatter x1, waiting for transfers between devices, body(): lax.psum_scatter(d_value_all, 'cp', scatter_dimension=1, tiled=True)  88.8 us
    dot_general x4, matrix products, masked_scores(): jnp.einsum('qhd,khd->hqk', q_three, k_three, preferred_element_type=jnp.f...  86.3 us
    convert_element_type x2, other arithmetic, attend_back(): d_scores = (probs * (d_probs - delta)).astype(jnp.bfloat16)  82.8 us
    psum x1, blocking collectives, body(): lax.psum((shards[0], shards[1], shards[2], shards[3], shards[4], shards[5...  82.4 us
    dot_general x2, matrix products, attend_back(): jnp.einsum('qhd,khd->hqk', d_three, v_three, preferred_element_type=jnp.f...  75.1 us
    all_gather x1, waiting for transfers between devices, body(): lax.all_gather(value_loc, 'cp', axis=1, tiled=True)  72.5 us
  transfers between devices with their start and end apart: 13, of which 10 were waited for; matrix products, arithmetic and copies ran while one was open for 17% of the time, Pallas kernels for 0%

commit v1 on v0

--- a/solution.py
+++ b/solution.py
@@ -253,22 +253,25 @@
         lax.psum_scatter(db_proj, "fsdp", scatter_dimension=0, tiled=True),
     )
     totals = lax.psum(
-        (
-            shards[0],
-            shards[1],
-            shards[2],
-            shards[3],
-            shards[4],
-            shards[5],
-            shards[6],
-            shards[7],
-            shards[8],
-            shards[9],
-            shards[10],
-            shards[11],
-            shards[12],
+        lax.psum(
+            (
+                shards[0],
+                shards[1],
+                shards[2],
+                shards[3],
+                shards[4],
+                shards[5],
+                shards[6],
+                shards[7],
+                shards[8],
+                shards[9],
+                shards[10],
+                shards[11],
+                shards[12],
+            ),
+            "rep",
         ),
-        ("cp", "rep"),
+        "cp",
     )
     return (
         layer_out,

time: 1500 us -> 1850 us (1.23)
  waiting for transfers between devices: 695 us -> 1090 us
  blocking collectives: 103 us -> 53.8 us
    psum x0 -> x1, waiting for transfers between devices: none -> 197 us  [body(): lax.psum(lax.psum((shards[0], shards[1], shards[2], shards[3], shards[4],...]
    psum x1, waiting for transfers between devices: 287 us -> 483 us  [body(): lax.psum((shards[0], shards[1], shards[2], shards[3], shards[4], shards[5...]
    psum x1, blocking collectives: 82.4 us -> 15.7 us  [body(): lax.psum((shards[0], shards[1], shards[2], shards[3], shards[4], shards[5...]
  transfers between devices with their start and end apart: 13 -> 14, of which waited for: 10 -> 11; matrix products, arithmetic and copies ran while one was open for 17% -> 14% of each run, Pallas kernels for 0% -> 0%
where the time goes in v1:
time: 1850 us
  waiting for transfers between devices  1090 us (59%)
  matrix products  411 us (22%)
  other arithmetic  160 us (9%)
  local copies, waits for them, and re-layouts  111 us (6%)
  blocking collectives  53.8 us (3%)
    psum x1, waiting for transfers between devices, body(): lax.psum((shards[0], shards[1], shards[2], shards[3], shards[4], shards[5...  483 us
    psum x1, waiting for transfers between devices, body(): lax.psum(lax.psum((shards[0], shards[1], shards[2], shards[3], shards[4],...  197 us
    reduce_scatter x1, waiting for transfers between devices, body(): lax.psum_scatter(d_key_all, 'cp', scatter_dimension=1, tiled=True)  122 us
    reduce_scatter x1, waiting for transfers between devices, body(): lax.psum_scatter(d_value_all, 'cp', scatter_dimension=1, tiled=True)  89 us
    dot_general x4, matrix products, masked_scores(): jnp.einsum('qhd,khd->hqk', q_three, k_three, preferred_element_type=jnp.f...  86.3 us
    convert_element_type x2, other arithmetic, attend_back(): d_scores = (probs * (d_probs - delta)).astype(jnp.bfloat16)  82.8 us
    dot_general x2, matrix products, attend_back(): jnp.einsum('qhd,khd->hqk', d_three, v_three, preferred_element_type=jnp.f...  75.1 us
    all_gather x1, waiting for transfers between devices, body(): lax.all_gather(value_loc, 'cp', axis=1, tiled=True)  72.5 us
  transfers between devices with their start and end apart: 14, of which 11 were waited for; matrix products, arithmetic and copies ran while one was open for 14% of the time, Pallas kernels for 0%

profile of v1, /device:TPU:0, one launch (start us, length us, event | category | flops | bytes accessed | tf_op | source)
XLA Modules:
  0.0 1845.9 jit_solution(9593175190271098832)
XLA Ops:
  25.0 6.0 add_convert_fusion
  50.2 56.3 %all-gather.20.cloned.1.call-done = bf16[2,2048,768]{1,2,0:T(8,128)(2,1)} async-done(((bf16[2,512,768]{1,2,0:T(8,128)(2,1)}), bf16[2,2048,768]{1,2,0:T(8,128)(2,1)}) %all-gather.20.cloned.1.call-update) | async-done | bytes 6291472 | tf_op jit(solution)/shard_map/all_gather | solution.py:89
  106.5 72.5 %all-gather.18.cloned.1.call-done = bf16[2,2048,768]{1,2,0:T(8,128)(2,1)} async-done(((bf16[2,512,768]{1,2,0:T(8,128)(2,1)}), bf16[2,2048,768]{1,2,0:T(8,128)(2,1)}) %all-gather.18.cloned.1.call-update) | async-done | bytes 6291472 | tf_op jit(solution)/shard_map/all_gather | solution.py:90
  178.9 155.5 %while.34 = (s32[]{:T(128)}, bf16[2,512,768]{2,1,0:T(8,128)(2,1)}, f32[2,12,512]{2,1,0:T(8,128)S(1)}, bf16[2,2048,768]{1,2,0:T(8,128)(2,1)}, s32[2,2048]{1,0:T(2...) while((s32[]{:T(128)}, bf16[2,512,768]{2,1,0:T(8,128)(2,1)}, ...), condition=%wide.region_5.6_spmd.clone, body=%wide.region_2.5_spmd.clone.sunk | while | flops 3375753728 | bytes 197388496 | solution.py:127
  183.3 5.4 constant_dynamic-slice_fusion.17
  188.6 23.9 %fusion.106 = (f32[12,512]{1,0:T(8,128)S(1)}, f32[12,512,2048]{2,1,0:T(8,128)}) fusion(pred[512,2048]{1,0:T(8,128)(4,1)} %fusion.105, bf16[512,12,64]{0,2,1:T(8,128)(2,1)} %bitcast.170, bf16[2048,12,64]{0,2,1:T(8,128)(2,1)S(1)} %bitcast.165), kind=kOutput, calls=%fused_computation.5.clone.1 | convolution fusion | flops 1648355328 | bytes 55336960 | tf_op jit(solution)/shard_map/while/body/eval_jaxpr/qhd,khd->hqk/dot_general | solution.py:99
  212.5 24.5 %fusion.107 = f32[12,512]{1,0:T(8,128)S(1)} fusion(f32[12,512,2048]{2,1,0:T(8,128)} %get-tuple-element.696, f32[12,512]{1,0:T(8,128)S(1)} %get-tuple-element.697, pred[512,2048]{1,0:T(8,128)(4,1)} %fusion.105), kind=kLoop, calls=%fused_computation.6.clone.1 | loop fusion | flops 50325504 | bytes 51429376 | tf_op jit(solution)/shard_map/while/body/eval_jaxpr/reduce_sum | solution.py:114
  237.1 20.2 %fusion.108 = bf16[12,64,512]{2,1,0:T(8,128)(2,1)S(1)} fusion(bf16[2048,12,64]{0,2,1:T(8,128)(2,1)S(1)} %bitcast.174, f32[12,512,2048]{2,1,0:T(8,128)} %get-tuple-element.696, f32[12,512]{1,0:T(8,128)S(1)} %fusion.107, f32[12,512]{1,0:T(8,128)S(1)} %get-tuple-element.697, pred[512,2048]{1,0:T(8,128)(4,1)S(1)} %copy-done), kind=kOutput, calls=%fused_computation.10.clone.1 | convolution fusion | flops 1673920512 | bytes 55361536 | tf_op jit(solution)/shard_map/while/body/eval_jaxpr/hqk,khd->qhd/dot_general | solution.py:116
  262.8 5.4 constant_dynamic-slice_fusion.17
  268.2 21.5 %fusion.106 = (f32[12,512]{1,0:T(8,128)S(1)}, f32[12,512,2048]{2,1,0:T(8,128)}) fusion(pred[512,2048]{1,0:T(8,128)(4,1)} %fusion.105, bf16[512,12,64]{0,2,1:T(8,128)(2,1)} %bitcast.170, bf16[2048,12,64]{0,2,1:T(8,128)(2,1)S(1)} %bitcast.165), kind=kOutput, calls=%fused_computation.5.clone.1 | convolution fusion | flops 1648355328 | bytes 55336960 | tf_op jit(solution)/shard_map/while/body/eval_jaxpr/qhd,khd->hqk/dot_general | solution.py:99
  289.7 22.9 %fusion.107 = f32[12,512]{1,0:T(8,128)S(1)} fusion(f32[12,512,2048]{2,1,0:T(8,128)} %get-tuple-element.696, f32[12,512]{1,0:T(8,128)S(1)} %get-tuple-element.697, pred[512,2048]{1,0:T(8,128)(4,1)} %fusion.105), kind=kLoop, calls=%fused_computation.6.clone.1 | loop fusion | flops 50325504 | bytes 51429376 | tf_op jit(solution)/shard_map/while/body/eval_jaxpr/reduce_sum | solution.py:114
  312.5 20.2 %fusion.108 = bf16[12,64,512]{2,1,0:T(8,128)(2,1)S(1)} fusion(bf16[2048,12,64]{0,2,1:T(8,128)(2,1)S(1)} %bitcast.174, f32[12,512,2048]{2,1,0:T(8,128)} %get-tuple-element.696, f32[12,512]{1,0:T(8,128)S(1)} %fusion.107, f32[12,512]{1,0:T(8,128)S(1)} %get-tuple-element.697, pred[512,2048]{1,0:T(8,128)(4,1)S(1)} %copy-done), kind=kOutput, calls=%fused_computation.10.clone.1 | convolution fusion | flops 1673920512 | bytes 55361536 | tf_op jit(solution)/shard_map/while/body/eval_jaxpr/hqk,khd->qhd/dot_general | solution.py:116
  338.9 11.0 fusion.43
  349.9 18.6 %convert_reduce_fusion = (f32[3072]{0:T(1024)}, bf16[1024,3072]{1,0:T(8,128)(2,1)S(1)}) fusion(bf16[1024,768]{1,0:T(8,128)(2,1)} %bitcast.176, bf16[3072,768]{1,0:T(8,128)(2,1)} %all-gather.26.cloned.1.call-done, f32[1024,3072]{1,0:T(8,128)} %fusion.43, f32[3072]{0:T(1024)S(1)} %bitcast.201), kind=kOutput, calls=%fused_computation.52 | convolution fusion | flops 4916769792 | bytes 25190400 | tf_op jit(solution)/shard_map/dot_general | solution.py:30
  368.5 6.1 multiply_reduce_fusion.1
  379.8 375.4 %while.35 = (s32[]{:T(128)}, bf16[2,512,768]{2,1,0:T(8,128)(2,1)}, f32[2,2048,768]{2,1,0:T(8,128)}, f32[2,2048,768]{2,1,0:T(8,128)}, bf16[2,2048,768]{1,2,0:T(8,...) while((s32[]{:T(128)}, bf16[2,512,768]{2,1,0:T(8,128)(2,1)}, ...), condition=%wide.region_12.13_spmd.clone, body=%wide.region_10.12_spmd.clone.sunk | while | flops 8247306752 | bytes 519514368 | solution.py:218
  392.8 20.5 %fusion.119 = f32[12,512,2048]{2,1,0:T(8,128)} fusion(bf16[512,12,64]{0,2,1:T(8,128)(2,1)} %bitcast.167, bf16[2048,12,64]{0,2,1:T(8,128)(2,1)S(1)} %bitcast.162), kind=kOutput, calls=%fused_computation.114.clone.1 | convolution fusion | flops 1610612736 | bytes 54263808 | tf_op jit(solution)/shard_map/while/body/eval_jaxpr/qhd,khd->hqk/dot_general | solution.py:99
  413.3 23.1 %fusion.121 = f32[12,64,2048]{2,1,0:T(8,128)} fusion(bf16[512,12,64]{0,2,1:T(8,128)(2,1)} %bitcast.172, f32[12,512,2048]{2,1,0:T(8,128)} %fusion.119, f32[12,512]{1,0:T(8,128)S(1)} %dynamic-slice_bitcast_fusion.2, pred[512,2048]{1,0:T(8,128)(4,1)} %fusion.120), kind=kOutput, calls=%fused_computation.24.clone.1 | convolution fusion | flops 1660944384 | bytes 58482688 | tf_op jit(solution)/shard_map/while/body/eval_jaxpr/hqk,qhd->khd/dot_general | solution.py:209
  436.4 6.6 copy.90
  443.1 37.6 %multiply_reduce_fusion.5 = (f32[12,512]{1,0:T(8,128)S(1)}, f32[12,512,2048]{2,1,0:T(8,128)}) fusion(f32[12,512,2048]{2,1,0:T(8,128)} %fusion.119, f32[12,512]{1,0:T(8,128)S(1)} %dynamic-slice_bitcast_fusion.2, pred[512,2048]{1,0:T(8,128)(4,1)} %fusion.120, bf16[512,12,64]{0,2,1:T(8,128)(2,1)} %bitcast.173, bf16[2048,12,64]{0,2,1:T(8,128)(2,1)} %bitcast.166), kind=kOutput, calls=%fused_computation.21.clone.1 | convolution fusion | flops 1673521152 | bytes 105693184 | tf_op jit(solution)/shard_map/while/body/eval_jaxpr/qhd,khd->hqk/dot_general | solution.py:188
  480.6 41.4 %multiply_convert_fusion.5 = bf16[12,512,2048]{2,1,0:T(8,128)(2,1)} fusion(f32[12,512,2048]{2,1,0:T(8,128)} %get-tuple-element.710, f32[12,512,2048]{2,1,0:T(8,128)} %fusion.119, f32[12,512]{1,0:T(8,128)S(1)} %get-tuple-element.711, f32[12,512]{1,0:T(8,128)S(1)} %dynamic-slice_bitcast_fusion.2, pred[512,2048]{1,0:T(8,128)(4,1)} %fusion.120), kind=kLoop, calls=%fused_computation.20.clone.1 | loop fusion | flops 75497472 | bytes 126926848 | tf_op jit(solution)/shard_map/while/body/eval_jaxpr/convert_element_type | solution.py:190
  522.0 13.4 convolution_multiply_fusion.4
  535.4 15.5 convolution_multiply_fusion.5
  551.0 6.6 copy.91
  558.8 10.2 constant_dynamic-update-slice_fusion.9
  578.9 20.5 %fusion.119 = f32[12,512,2048]{2,1,0:T(8,128)} fusion(bf16[512,12,64]{0,2,1:T(8,128)(2,1)} %bitcast.167, bf16[2048,12,64]{0,2,1:T(8,128)(2,1)S(1)} %bitcast.162), kind=kOutput, calls=%fused_computation.114.clone.1 | convolution fusion | flops 1610612736 | bytes 54263808 | tf_op jit(solution)/shard_map/while/body/eval_jaxpr/qhd,khd->hqk/dot_general | solution.py:99
  599.4 23.1 %fusion.121 = f32[12,64,2048]{2,1,0:T(8,128)} fusion(bf16[512,12,64]{0,2,1:T(8,128)(2,1)} %bitcast.172, f32[12,512,2048]{2,1,0:T(8,128)} %fusion.119, f32[12,512]{1,0:T(8,128)S(1)} %dynamic-slice_bitcast_fusion.2, pred[512,2048]{1,0:T(8,128)(4,1)} %fusion.120), kind=kOutput, calls=%fused_computation.24.clone.1 | convolution fusion | flops 1660944384 | bytes 58482688 | tf_op jit(solution)/shard_map/while/body/eval_jaxpr/hqk,qhd->khd/dot_general | solution.py:209
  622.5 6.6 copy.90
  629.2 37.6 %multiply_reduce_fusion.5 = (f32[12,512]{1,0:T(8,128)S(1)}, f32[12,512,2048]{2,1,0:T(8,128)}) fusion(f32[12,512,2048]{2,1,0:T(8,128)} %fusion.119, f32[12,512]{1,0:T(8,128)S(1)} %dynamic-slice_bitcast_fusion.2, pred[512,2048]{1,0:T(8,128)(4,1)} %fusion.120, bf16[512,12,64]{0,2,1:T(8,128)(2,1)} %bitcast.173, bf16[2048,12,64]{0,2,1:T(8,128)(2,1)} %bitcast.166), kind=kOutput, calls=%fused_computation.21.clone.1 | convolution fusion | flops 1673521152 | bytes 105693184 | tf_op jit(solution)/shard_map/while/body/eval_jaxpr/qhd,khd->hqk/dot_general | solution.py:188
  666.8 41.4 %multiply_convert_fusion.5 = bf16[12,512,2048]{2,1,0:T(8,128)(2,1)} fusion(f32[12,512,2048]{2,1,0:T(8,128)} %get-tuple-element.710, f32[12,512,2048]{2,1,0:T(8,128)} %fusion.119, f32[12,512]{1,0:T(8,128)S(1)} %get-tuple-element.711, f32[12,512]{1,0:T(8,128)S(1)} %dynamic-slice_bitcast_fusion.2, pred[512,2048]{1,0:T(8,128)(4,1)} %fusion.120), kind=kLoop, calls=%fused_computation.20.clone.1 | loop fusion | flops 75497472 | bytes 126926848 | tf_op jit(solution)/shard_map/while/body/eval_jaxpr/convert_element_type | solution.py:190
  708.1 13.4 convolution_multiply_fusion.4
  721.5 15.5 convolution_multiply_fusion.5
  737.1 6.6 copy.91
  745.0 10.1 constant_dynamic-update-slice_fusion.9
  761.1 11.7 fusion.42
  774.1 13.0 fusion.44
  787.2 89.0 %reduce-scatter.9.cloned.1.call-done = f32[2,512,768]{2,1,0:T(8,128)} async-done(((f32[2,2048,768]{2,1,0:T(8,128)}), f32[2,512,768]{2,1,0:T(8,128)}) %reduce-scatter.9.cloned.1.call-update) | async-done | bytes 3145744 | tf_op jit(solution)/shard_map/reduce_scatter | solution.py:223
  878.2 121.8 %reduce-scatter.7.cloned.1.call-done = f32[2,512,768]{2,1,0:T(8,128)} async-done(((f32[2,2048,768]{2,1,0:T(8,128)}), f32[2,512,768]{2,1,0:T(8,128)}) %reduce-scatter.7.cloned.1.call-update) | async-done | bytes 3145744 | tf_op jit(solution)/shard_map/reduce_scatter | solution.py:222
  1003.4 8.3 fusion.39
  1012.8 21.2 %reduce-scatter.15.cloned.1.call-done = f32[384,3072]{1,0:T(8,128)} async-done(((f32[768,3072]{1,0:T(8,128)}), f32[384,3072]{1,0:T(8,128)}) %reduce-scatter.15.cloned.1.call-update) | async-done | bytes 4718608 | tf_op jit(solution)/shard_map/reduce_scatter | solution.py:250
  1034.0 21.5 %reduce-scatter.17.cloned.1.call-done = f32[1536,768]{1,0:T(8,128)} async-done(((f32[3072,768]{1,0:T(8,128)}), f32[1536,768]{1,0:T(8,128)}) %reduce-scatter.17.cloned.1.call-update) | async-done | bytes 4718608 | tf_op jit(solution)/shard_map/reduce_scatter | solution.py:252
  1055.5 19.1 %reduce-scatter.11.cloned.1.call-done = f32[384,2304]{1,0:T(8,128)} async-done(((f32[768,2304]{1,0:T(8,128)}), f32[384,2304]{1,0:T(8,128)}) %reduce-scatter.11.cloned.1.call-update) | async-done | bytes 3538960 | tf_op jit(solution)/shard_map/reduce_scatter | solution.py:243
  1074.7 482.9 %all-reduce.17.cloned.1.call-done = (f32[384,2304]{1,0:T(8,128)}, f32[384,768]{1,0:T(8,128)}, f32[384,3072]{1,0:T(8,128)}, f32[1536,768]{1,0:T(8,128)}) async-done(((f32[384,2304]{1,0:T(8,128)}, f32[384,768]{1,0:T(8,128)}, f32[384,3072]{1,0:T(8,128)}, f32[1536,768]{1,0:T(8,128)}), (f32[384,2304]{1,0:T(8,128)}, f32[384,768]{1,0:T(8,128)}, f32[384,3072]{1,0:T(8,128)}, ...) | async-done | bytes 14155792 | tf_op jit(solution)/shard_map/psum | solution.py:256
  1562.5 14.7 add_convert_fusion.2
  1577.2 5.5 fusion.45
  1592.5 15.7 all-reduce.9
  1608.2 17.9 all-reduce.11
  1631.1 197.3 %all-reduce.19.cloned.1.call-done = (f32[384,2304]{1,0:T(8,128)}, f32[384,768]{1,0:T(8,128)}, f32[384,3072]{1,0:T(8,128)}, f32[1536,768]{1,0:T(8,128)}) async-done(((f32[384,2304]{1,0:T(8,128)}, f32[384,768]{1,0:T(8,128)}, f32[384,3072]{1,0:T(8,128)}, f32[1536,768]{1,0:T(8,128)}), (f32[384,2304]{1,0:T(8,128)}, f32[384,768]{1,0:T(8,128)}, f32[384,3072]{1,0:T(8,128)}, ...) | async-done | bytes 14155792 | tf_op jit(solution)/shard_map/psum | solution.py:255
  (299 shorter events, 121.9 us)
Async XLA Ops:
  7.2 12.8 copy-start.4
  7.2 17.8 all-gather.16.cloned.1.call-start
  7.9 98.5 %all-gather.20.cloned.1.call-start = ((), (), s32[]{:S(2)}) async-start(), calls=%async_computation.8 | async-start | bytes 7864320 | tf_op jit(solution)/shard_map/all_gather | solution.py:89
  10.6 20.4 %copy-start.30 = (f32[768]{0:T(1024)}, f32[768]{0:T(1024)S(1)}, u32[]{:S(2)}) copy-start(f32[768]{0:T(1024)S(1)} %reshape.445) | copy-start | bytes 9220
  21.9 9.2 copy-start.19
  35.1 143.8 %all-gather.18.cloned.1.call-start = ((), (), s32[]{:S(2)}) async-start(), calls=%async_computation.7 | async-start | bytes 7864320 | tf_op jit(solution)/shard_map/all_gather | solution.py:90
  36.8 6.7 copy-start.52
  36.8 9.1 copy-start.47
  36.8 297.7 %all-gather.22.cloned.1.call-start = ((), (), s32[]{:S(2)}) async-start(), calls=%async_computation.9 | async-start | bytes 1769472 | tf_op jit(solution)/shard_map/all_gather | solution.py:65
  37.4 141.6 %copy-start.23 = (s32[2,2048]{1,0:T(2,128)S(1)}, s32[2,2048]{1,0:T(2,128)}, u32[]{:S(2)}) copy-start(s32[2,2048]{1,0:T(2,128)} %param.21) | copy-start | bytes 49156
  37.4 301.5 %all-gather.24.cloned.1.call-start = ((), (), s32[]{:S(2)}) async-start(), calls=%async_computation.10 | async-start | bytes 7077888 | tf_op jit(solution)/shard_map/all_gather | solution.py:69
  38.0 311.9 %all-gather.26.cloned.1.call-start = ((), (), s32[]{:S(2)}) async-start(), calls=%async_computation.11 | async-start | bytes 7077888 | tf_op jit(solution)/shard_map/all_gather | solution.py:71
  38.5 837.6 %reduce-scatter.9.cloned.1.call-start = ((), (), s32[]{:S(2)}) async-start(), calls=%async_computation.13 | async-start | bytes 15728640 | tf_op jit(solution)/shard_map/reduce_scatter | solution.py:223
  178.9 155.5 %copy-start.46 = (f32[768]{0:T(1024)S(1)}, f32[768]{0:T(1024)}, u32[]{:S(2)}) copy-start(f32[768]{0:T(1024)} %reshape.447) | copy-start | bytes 9220
  212.5 24.5 %copy-start = (pred[512,2048]{1,0:T(8,128)(4,1)S(1)}, pred[512,2048]{1,0:T(8,128)(4,1)}, u32[]{:S(2)}) copy-start(pred[512,2048]{1,0:T(8,128)(4,1)} %fusion.105) | copy-start | bytes 3145732 | tf_op jit(solution)/shard_map/while
  212.5 24.5 %copy-start.3 = (bf16[1,2048,768]{1,2,0:T(8,128)(2,1)S(1)}, bf16[1,2048,768]{1,2,0:T(8,128)(2,1)}, u32[]{:S(2)}) copy-start(bf16[1,2048,768]{1,2,0:T(8,128)(2,1)} %get-tuple-element.694) | copy-start | bytes 9437188 | tf_op jit(solution)/shard_map/while
  289.6 22.9 %copy-start = (pred[512,2048]{1,0:T(8,128)(4,1)S(1)}, pred[512,2048]{1,0:T(8,128)(4,1)}, u32[]{:S(2)}) copy-start(pred[512,2048]{1,0:T(8,128)(4,1)} %fusion.105) | copy-start | bytes 3145732 | tf_op jit(solution)/shard_map/while
  289.6 22.9 %copy-start.3 = (bf16[1,2048,768]{1,2,0:T(8,128)(2,1)S(1)}, bf16[1,2048,768]{1,2,0:T(8,128)(2,1)}, u32[]{:S(2)}) copy-start(bf16[1,2048,768]{1,2,0:T(8,128)(2,1)} %get-tuple-element.694) | copy-start | bytes 9437188 | tf_op jit(solution)/shard_map/while
  338.3 36.4 %copy-start.6 = (f32[1024,768]{1,0:T(8,128)}, f32[1024,768]{1,0:T(8,128)S(1)}, u32[]{:S(2)}) copy-start(f32[1024,768]{1,0:T(8,128)S(1)} %get-tuple-element.565) | copy-start | bytes 9437188
  338.3 36.4 %copy-start.24 = (f32[1024]{0:T(1024)}, f32[1024]{0:T(1024)S(1)}, u32[]{:S(2)}) copy-start(f32[1024]{0:T(1024)S(1)} %broadcast_multiply_fusion) | copy-start | bytes 12292
  338.8 35.9 %copy-start.26 = (f32[1024]{0:T(1024)}, f32[1024]{0:T(1024)S(1)}, u32[]{:S(2)}) copy-start(f32[1024]{0:T(1024)S(1)} %fusion.36) | copy-start | bytes 12292
  338.8 11.1 copy-start.43
  349.9 18.6 %copy-start.54 = (bf16[768,3072]{1,0:T(8,128)(2,1)S(1)}, bf16[768,3072]{1,0:T(8,128)(2,1)}, u32[]{:S(2)}) copy-start(bf16[768,3072]{1,0:T(8,128)(2,1)} %all-gather.24.cloned.1.call-done) | copy-start | bytes 14155780
  368.5 6.1 copy-start.14
  383.0 9.6 copy-start.12
  386.4 6.2 copy-start.1
  551.0 6.6 copy-start.2
  558.8 10.2 copy-start.13
  569.1 9.6 copy-start.12
  572.5 6.2 copy-start.1
  737.1 6.6 copy-start.2
  744.9 10.1 copy-start.13
  755.2 244.8 %reduce-scatter.7.cloned.1.call-start = ((), (), s32[]{:S(2)}) async-start(), calls=%async_computation.12 | async-start | bytes 15728640 | tf_op jit(solution)/shard_map/reduce_scatter | solution.py:222
  756.0 256.8 %reduce-scatter.13.cloned.1.call-start = ((), (), s32[]{:S(2)}) async-start(), calls=%async_computation.15 | async-start | bytes 3538944 | tf_op jit(solution)/shard_map/reduce_scatter | solution.py:246
  761.0 273.0 %reduce-scatter.15.cloned.1.call-start = ((), (), s32[]{:S(2)}) async-start(), calls=%async_computation.16 | async-start | bytes 14155776 | tf_op jit(solution)/shard_map/reduce_scatter | solution.py:250
  772.7 282.7 %reduce-scatter.17.cloned.1.call-start = ((), (), s32[]{:S(2)}) async-start(), calls=%async_computation.17 | async-start | bytes 14155776 | tf_op jit(solution)/shard_map/reduce_scatter | solution.py:252
  787.1 287.5 %reduce-scatter.11.cloned.1.call-start = ((), (), s32[]{:S(2)}) async-start(), calls=%async_computation.14 | async-start | bytes 10616832 | tf_op jit(solution)/shard_map/reduce_scatter | solution.py:243
  878.2 133.5 %copy-start.15 = (bf16[2,512,768]{2,1,0:T(8,128)(2,1)}, bf16[2,512,768]{2,1,0:T(8,128)(2,1)S(1)}, u32[]{:S(2)}) copy-start(bf16[2,512,768]{2,1,0:T(8,128)(2,1)S(1)} %convert.15) | copy-start | bytes 4718596
  1011.7 545.8 %all-reduce.17.cloned.1.call-start = ((), (), s32[]{:S(2)}) async-start(), calls=%async_computation.18 | async-start | bytes 28311552 | tf_op jit(solution)/shard_map/psum | solution.py:256
  1074.6 753.7 %all-reduce.19.cloned.1.call-start = ((), (), s32[]{:S(2)}) async-start(), calls=%async_computation.19 | async-start | bytes 28311552 | tf_op jit(solution)/shard_map/psum | solution.py:255
  1562.4 14.8 copy-start.5
  1562.4 14.8 copy-start.16
  1562.4 14.8 copy-start.18
  1562.4 14.8 copy-start.31
  1562.4 14.8 copy-start.35
  1562.5 14.8 copy-start.55
  1577.2 5.6 copy-start.41
  1586.2 40.0 %copy-start.39 = (f32[1024]{0:T(1024)S(1)}, f32[1024]{0:T(1024)}, u32[]{:S(2)}) copy-start(f32[1024]{0:T(1024)} %copy-done.38) | copy-start | bytes 12292
  (34 other events, 100.9 us)
Sparse Core Ops, SparseCore 0:
  9.6 15.3 all-gather.15
  35.2 71.1 all-gather.19
  108.9 70.0 all-gather.17
  180.3 9.2 all-gather.21
  191.0 15.5 all-gather.23
  208.0 15.6 all-gather.25
  755.3 120.7 reduce-scatter.8
  879.3 120.7 reduce-scatter.6
  1002.9 9.8 reduce-scatter.12
  1015.0 18.9 reduce-scatter.14
  1036.4 19.0 reduce-scatter.16
  1057.7 16.8 reduce-scatter.10
  1077.5 479.9 all-reduce.16
  1561.3 266.9 all-reduce.18
